TPU v7x, 128 devices: a whole 4x4x4 slice. The times are simulated.
128 devices in a mesh: walker: 16 (over x, y_hi, core), prow: 2 (over y_lo), pcol: 4 (over z).
Axes of the slice: x: 4, y: 4 (y_hi: 2, y_lo: 2; y = y_hi * 2 + y_lo), z: 4, core: 2. Of those that a mesh axis runs over, the one named last changes fastest.
Arguments:
- o_rows: bfloat16 [32768, 2048], P('walker', ('prow', 'pcol')), may hold values from -21 to 21
- o_cols: bfloat16 [32768, 4096], P('walker', ('pcol', 'prow')), may hold values from -48 to 48
- grad_energy: bfloat16 [32768, 4096], P('walker', ('pcol', 'prow')), may hold values from -8 to 8
- energy: float32 [32768], P('walker'), may hold values from -5 to 1
Outputs:
- hamil: float32 [2048, 4096], P(('prow', 'walker'), 'pcol')
- correlation: float32 [2048, 4096], P(('prow', 'walker'), 'pcol')
All inputs are finite; a program needn't handle non-finite values.
Results may differ from a plain program's by a relative error of at most 0.008.
Values may be sent and summed in bfloat16 or wider, within the bound.
A program may use at most 128 MiB of HBM per device.

v0:
```python
import jax
import jax.numpy as jnp
from jax import lax
from jax.sharding import PartitionSpec as P


def column_sums(values):
    return jnp.sum(values.astype(jnp.float32), axis=0)


def tile_product(row_tile, right_tile):
    return lax.dot_general(
        row_tile, right_tile, (((0,), (0,)), ((), ())), preferred_element_type=jnp.float32
    )


def per_device(o_rows, o_cols, grad_energy, energy):
    count = energy.shape[0] * lax.axis_size("walker")
    row_total, col_total = lax.psum((column_sums(o_rows), column_sums(o_cols)), "walker")
    row_shard = (o_rows - row_total / count).astype(jnp.bfloat16)
    col_shard = (o_cols - col_total / count).astype(jnp.bfloat16)
    row_tile = lax.all_gather(row_shard, "pcol", axis=1, tiled=True)
    col_tile, grad_tile = (
        lax.all_gather(col_shard, "prow", axis=1, tiled=True),
        lax.all_gather(grad_energy, "prow", axis=1, tiled=True),
    )
    weighted = (energy[:, None] * col_tile + grad_tile).astype(jnp.bfloat16)
    paired = jnp.concatenate((col_tile, weighted), axis=1)
    summed = lax.psum_scatter(
        tile_product(row_tile, paired), "walker", scatter_dimension=0, tiled=True
    )
    width = col_tile.shape[1]
    correlation = summed[:, :width]
    hamil = summed[:, width:]
    return (hamil / count, correlation / count)


def solution(mesh):
    in_specs = (
        P("walker", ("prow", "pcol")),
        P("walker", ("pcol", "prow")),
        P("walker", ("pcol", "prow")),
        P("walker"),
    )
    out_specs = (P(("prow", "walker"), "pcol"), P(("prow", "walker"), "pcol"))
    return jax.shard_map(
        per_device, mesh=mesh, in_specs=in_specs, out_specs=out_specs, check_vma=False
    )
```

profile of v0, /device:TPU:0, one launch (start us, length us, event | category | flops | bytes accessed | tf_op | source)
XLA Modules:
  0.0 314.8 jit_solution(17419922395982080322)
XLA Ops:
  7.2 0.0 copy-start
  7.2 0.0 all-gather.8.cloned.1.call-start
  7.2 0.7 all-gather.8.cloned.1.call-update
  7.9 0.0 all-gather.6.cloned.1.call-start
  8.0 1.5 convert_reduce_fusion.1
  9.5 0.0 copy-done
  9.5 0.0 copy-start.1
  9.5 0.3 convert_reduce_fusion
  9.8 38.7 %all-reduce = (f32[256]{0:T(256)S(1)}, f32[512]{0:T(512)S(1)}) all-reduce(f32[256]{0:T(256)S(1)} %convert_reduce_fusion.1, f32[512]{0:T(512)S(1)} %convert_reduce_fusion), channel_id=1, replica_groups=mesh['walker'=16,'prow'=2,'pcol'=4] {'walker'}, use_global_device_ids=true, to_apply=%region_1.0 | all-reduce | flops 768 | bytes 6144 | tf_op jit(solution)/shard_map/psum | solution.py:19
  48.5 0.0 copy-start.2
  48.5 1.8 fusion.4
  50.3 0.0 all-gather.6.cloned.1.call-update
  50.3 0.0 all-gather.4.cloned.1.call-start
  50.4 0.0 copy-done.1
  50.4 1.2 fusion.5
  51.6 0.0 all-gather.4.cloned.1.call-update
  51.6 0.0 reduce-scatter.2.cloned.1.call-start
  51.7 20.1 %all-gather.8.cloned.1.call-done = bf16[2048,1024]{1,0:T(8,128)(2,1)} async-done(((bf16[2048,512]{1,0:T(8,128)(2,1)}), bf16[2048,1024]{1,0:T(8,128)(2,1)}) %all-gather.8.cloned.1.call-update) | async-done | bytes 4194320 | tf_op jit(solution)/shard_map/all_gather | solution.py:25
  71.8 61.9 %all-gather.6.cloned.1.call-done = bf16[2048,1024]{1,0:T(8,128)(2,1)} async-done(((bf16[2048,512]{1,0:T(8,128)(2,1)}), bf16[2048,1024]{1,0:T(8,128)(2,1)}) %all-gather.6.cloned.1.call-update) | async-done | bytes 4194320 | tf_op jit(solution)/shard_map/all_gather | solution.py:24
  133.7 0.0 copy-done.2
  133.7 5.4 %add_convert_fusion = bf16[2048,1024]{1,0:T(8,128)(2,1)} fusion(bf16[2048,1024]{1,0:T(8,128)(2,1)} %all-gather.8.cloned.1.call-done, bf16[2048,1024]{1,0:T(8,128)(2,1)} %all-gather.6.cloned.1.call-done, f32[2048]{0:T(1024)S(1)} %copy-done.2), kind=kLoop, calls=%fused_computation.4 | loop fusion | flops 10485760 | bytes 12591104 | tf_op jit(solution)/shard_map/convert_element_type | solution.py:27
  139.1 48.8 %all-gather.4.cloned.1.call-done = bf16[2048,1024]{1,0:T(8,128)(2,1)} async-done(((bf16[2048,256]{1,0:T(8,128)(2,1)}), bf16[2048,1024]{1,0:T(8,128)(2,1)}) %all-gather.4.cloned.1.call-update) | async-done | bytes 4194320 | tf_op jit(solution)/shard_map/all_gather | solution.py:22
  187.9 15.2 %fusion = f32[1024,2048]{1,0:T(8,128)} fusion(bf16[2048,1024]{1,0:T(8,128)(2,1)} %all-gather.4.cloned.1.call-done, bf16[2048,1024]{1,0:T(8,128)(2,1)} %add_convert_fusion, bf16[2048,1024]{1,0:T(8,128)(2,1)} %all-gather.6.cloned.1.call-done), kind=kOutput, calls=%fused_computation | convolution fusion | flops 8606711808 | bytes 20971520 | tf_op jit(solution)/shard_map/dot_general | solution.py:12
  203.1 0.0 reduce-scatter.2.cloned.1.call-update
  203.1 103.3 %reduce-scatter.2.cloned.1.call-done = f32[64,2048]{1,0:T(8,128)} async-done(((f32[1024,2048]{1,0:T(8,128)}), f32[64,2048]{1,0:T(8,128)}) %reduce-scatter.2.cloned.1.call-update) | async-done | bytes 524304 | tf_op jit(solution)/shard_map/reduce_scatter | solution.py:29
  306.4 1.9 slice_multiply_fusion
  (2 shorter events, 0.0 us)
Async XLA Ops:
  7.2 2.3 copy-start
  7.2 64.6 %all-gather.8.cloned.1.call-start = ((), (), s32[]{:S(2)}) async-start(), calls=%async_computation.3 | async-start | bytes 6291456 | tf_op jit(solution)/shard_map/all_gather | solution.py:25
  7.9 125.8 %all-gather.6.cloned.1.call-start = ((), (), s32[]{:S(2)}) async-start(), calls=%async_computation.2 | async-start | bytes 6291456 | tf_op jit(solution)/shard_map/all_gather | solution.py:24
  9.5 40.9 %copy-start.1 = (bf16[2048,256]{1,0:T(8,128)(2,1)S(1)}, bf16[2048,256]{1,0:T(8,128)(2,1)}, u32[]{:S(2)}) copy-start(bf16[2048,256]{1,0:T(8,128)(2,1)} %param.4) | copy-start | bytes 3145732
  48.5 85.1 %copy-start.2 = (f32[2048]{0:T(1024)S(1)}, f32[2048]{0:T(1024)}, u32[]{:S(2)}) copy-start(f32[2048]{0:T(1024)} %param.7) | copy-start | bytes 24580
  50.3 137.6 %all-gather.4.cloned.1.call-start = ((), (), s32[]{:S(2)}) async-start(), calls=%async_computation.1 | async-start | bytes 5242880 | tf_op jit(solution)/shard_map/all_gather | solution.py:22
  51.6 254.8 %reduce-scatter.2.cloned.1.call-start = ((), (), s32[]{:S(2)}) async-start(), calls=%async_computation.4 | async-start | bytes 8912896 | tf_op jit(solution)/shard_map/reduce_scatter | solution.py:29
Sparse Core Ops, SparseCore 0:
  9.6 62.1 all-gather.7
  73.5 60.1 all-gather.5
  135.3 52.5 all-gather.3
  203.2 103.1 reduce-scatter.1
where the time goes:
time: 315 us
  waiting for transfers between devices  235 us (75%)
  blocking collectives  38.7 us (12%)
  matrix products  15.2 us (5%)
  between operations  13.8 us (4%)
  other arithmetic  12.2 us (4%)
    reduce_scatter x1, waiting for transfers between devices, per_device(): lax.psum_scatter(tile_product(row_tile, paired), 'walker', scatter_dimens...  103 us
    all_gather x1, waiting for transfers between devices, per_device(): lax.all_gather(col_shard, 'prow', axis=1, tiled=True)  61.9 us
    all_gather x1, waiting for transfers between devices, per_device(): row_tile = lax.all_gather(row_shard, 'pcol', axis=1, tiled=True)  48.8 us
    psum x1, blocking collectives, per_device(): lax.psum((column_sums(o_rows), column_sums(o_cols)), 'walker')  38.7 us
    all_gather x1, waiting for transfers between devices, per_device(): lax.all_gather(grad_energy, 'prow', axis=1, tiled=True)  20.1 us
    dot_general x1, matrix products, tile_product(): lax.dot_general(row_tile, right_tile, (((0,), (0,)), ((), ())), preferred...  15.2 us
  transfers between devices with their start and end apart: 4, of which 4 were waited for; matrix products, arithmetic and copies ran while one was open for 3% of the time, Pallas kernels for 0%

commit v1 on v0

--- a/solution.py
+++ b/solution.py
@@ -2,6 +2,14 @@
 import jax.numpy as jnp
 from jax import lax
 from jax.sharding import PartitionSpec as P
+
+
+def connect_the_things(out_dim, load):
+    blocks_here = []
+    for _ in range(lax.psum(1, "prow")):
+        blocks_here.append(load)
+    a_now = jnp.concatenate(lax.all_to_all(jnp.stack(blocks_here, 0), "prow", 0, 0), out_dim)
+    return a_now
 
 
 def column_sums(values):
@@ -21,7 +29,7 @@
     col_shard = (o_cols - col_total / count).astype(jnp.bfloat16)
     row_tile = lax.all_gather(row_shard, "pcol", axis=1, tiled=True)
     col_tile, grad_tile = (
-        lax.all_gather(col_shard, "prow", axis=1, tiled=True),
+        connect_the_things(1, col_shard),
         lax.all_gather(grad_energy, "prow", axis=1, tiled=True),
     )
     weighted = (energy[:, None] * col_tile + grad_tile).astype(jnp.bfloat16)

time: 315 us -> 278 us (0.88)
  waiting for transfers between devices: 235 us -> 130 us
  blocking collectives: 38.7 us -> 105 us
    all_to_all x0 -> x1, blocking collectives: none -> 65.9 us  [connect_the_things(): lax.all_to_all(jnp.stack(blocks_here, 0), 'prow', 0, 0)]
    all_gather x1 -> x0, waiting for transfers between devices: 61.9 us -> none  [per_device(): lax.all_gather(col_shard, 'prow', axis=1, tiled=True)]
    all_gather x1, waiting for transfers between devices: 48.8 us -> 26.3 us  [per_device(): row_tile = lax.all_gather(row_shard, 'pcol', axis=1, tiled=True)]
    all_gather x1, waiting for transfers between devices: 20.1 us -> 0.01 us  [per_device(): lax.all_gather(grad_energy, 'prow', axis=1, tiled=True)]
  transfers between devices with their start and end apart: 4 -> 3, of which waited for: 4 -> 2; matrix products, arithmetic and copies ran while one was open for 3% -> 4% of each run, Pallas kernels for 0% -> 0%
where the time goes in v1:
time: 278 us
  waiting for transfers between devices  130 us (47%)
  blocking collectives  105 us (38%)
  matrix products  15.2 us (5%)
  between operations  13.8 us (5%)
  other arithmetic  11.2 us (4%)
    reduce_scatter x1, waiting for transfers between devices, per_device(): lax.psum_scatter(tile_product(row_tile, paired), 'walker', scatter_dimens...  103 us
    all_to_all x1, blocking collectives, connect_the_things(): lax.all_to_all(jnp.stack(blocks_here, 0), 'prow', 0, 0)  65.9 us
    psum x1, blocking collectives, per_device(): lax.psum((column_sums(o_rows), column_sums(o_cols)), 'walker')  38.7 us
    all_gather x1, waiting for transfers between devices, per_device(): row_tile = lax.all_gather(row_shard, 'pcol', axis=1, tiled=True)  26.3 us
    dot_general x1, matrix products, tile_product(): lax.dot_general(row_tile, right_tile, (((0,), (0,)), ((), ())), preferred...  15.2 us
  transfers between devices with their start and end apart: 3, of which 2 were waited for; matrix products, arithmetic and copies ran while one was open for 4% of the time, Pallas kernels for 0%

profile of v1, /device:TPU:0, one launch (start us, length us, event | category | flops | bytes accessed | tf_op | source)
XLA Modules:
  0.0 277.8 jit_solution(1935094033432115249)
XLA Ops:
  7.2 0.0 copy-start.1
  7.2 0.0 copy-start
  7.2 0.0 all-gather.5.cloned.1.call-start
  7.2 0.7 all-gather.5.cloned.1.call-update
  7.9 0.0 all-gather.3.cloned.1.call-start
  8.0 1.5 convert_reduce_fusion.1
  9.5 0.0 copy-done
  9.5 0.3 convert_reduce_fusion
  9.8 38.7 %all-reduce = (f32[256]{0:T(256)S(1)}, f32[512]{0:T(512)S(1)}) all-reduce(f32[256]{0:T(256)S(1)} %convert_reduce_fusion.1, f32[512]{0:T(512)S(1)} %convert_reduce_fusion), channel_id=1, replica_groups=mesh['walker'=16,'prow'=2,'pcol'=4] {'walker'}, use_global_device_ids=true, to_apply=%region_1.0 | all-reduce | flops 768 | bytes 6144 | tf_op jit(solution)/shard_map/psum | solution.py:27
  48.5 0.0 copy-done.1
  48.5 1.2 fusion.5
  49.7 0.0 all-gather.3.cloned.1.call-update
  49.8 0.0 reduce-scatter.2.cloned.1.call-start
  49.8 0.4 fusion.6
  50.2 0.4 pad_maximum_fusion
  50.6 65.9 %all_to_all.5 = bf16[2,2048,512]{2,1,0:T(8,128)(2,1)S(1)} all-to-all(bf16[2,2048,512]{2,1,0:T(8,128)(2,1)S(1)} %pad_maximum_fusion), channel_id=1, replica_groups=mesh['walker'=16,'prow'=2,'pcol'=4] {'prow'}, dimensions={0} | all-to-all | bytes 8388608 | tf_op jit(solution)/shard_map/all_to_all | solution.py:11
  116.5 0.0 copy-start.2
  116.5 2.6 copy.7
  119.1 0.0 all-gather.5.cloned.1.call-done
  119.1 0.0 copy-done.2
  119.1 5.5 %add_convert_fusion = bf16[2048,1024]{1,0:T(8,128)(2,1)} fusion(bf16[2048,1024]{1,0:T(8,128)(2,1)} %all-gather.5.cloned.1.call-done, bf16[2048,1024]{1,0:T(8,128)(2,1)} %bitcast.7, f32[2048]{0:T(1024)S(1)} %copy-done.2), kind=kLoop, calls=%fused_computation.4 | loop fusion | flops 10485760 | bytes 12591104 | tf_op jit(solution)/shard_map/convert_element_type | solution.py:35
  124.6 26.3 %all-gather.3.cloned.1.call-done = bf16[2048,1024]{1,0:T(8,128)(2,1)} async-done(((bf16[2048,256]{1,0:T(8,128)(2,1)}), bf16[2048,1024]{1,0:T(8,128)(2,1)}) %all-gather.3.cloned.1.call-update) | async-done | bytes 4194320 | tf_op jit(solution)/shard_map/all_gather | solution.py:30
  150.9 15.2 %fusion = f32[1024,2048]{1,0:T(8,128)} fusion(bf16[2048,1024]{1,0:T(8,128)(2,1)} %all-gather.3.cloned.1.call-done, bf16[2048,1024]{1,0:T(8,128)(2,1)} %add_convert_fusion, bf16[2048,1024]{1,0:T(8,128)(2,1)} %bitcast.8), kind=kOutput, calls=%fused_computation | convolution fusion | flops 8606711808 | bytes 20971520 | tf_op jit(solution)/shard_map/dot_general | solution.py:20
  166.1 0.0 reduce-scatter.2.cloned.1.call-update
  166.1 103.3 %reduce-scatter.2.cloned.1.call-done = f32[64,2048]{1,0:T(8,128)} async-done(((f32[1024,2048]{1,0:T(8,128)}), f32[64,2048]{1,0:T(8,128)}) %reduce-scatter.2.cloned.1.call-update) | async-done | bytes 524304 | tf_op jit(solution)/shard_map/reduce_scatter | solution.py:37
  269.4 1.9 slice_multiply_fusion
  (2 shorter events, 0.0 us)
Async XLA Ops:
  7.2 41.4 %copy-start.1 = (bf16[2048,256]{1,0:T(8,128)(2,1)S(1)}, bf16[2048,256]{1,0:T(8,128)(2,1)}, u32[]{:S(2)}) copy-start(bf16[2048,256]{1,0:T(8,128)(2,1)} %param.4) | copy-start | bytes 3145732
  7.2 2.3 copy-start
  7.2 111.9 %all-gather.5.cloned.1.call-start = ((), (), s32[]{:S(2)}) async-start(), calls=%async_computation.3 | async-start | bytes 6291456 | tf_op jit(solution)/shard_map/all_gather | solution.py:33
  7.9 143.0 %all-gather.3.cloned.1.call-start = ((), (), s32[]{:S(2)}) async-start(), calls=%async_computation.2 | async-start | bytes 5242880 | tf_op jit(solution)/shard_map/all_gather | solution.py:30
  49.8 219.6 %reduce-scatter.2.cloned.1.call-start = ((), (), s32[]{:S(2)}) async-start(), calls=%async_computation.4 | async-start | bytes 8912896 | tf_op jit(solution)/shard_map/reduce_scatter | solution.py:37
  116.5 2.6 copy-start.2
Sparse Core Ops, SparseCore 0:
  9.6 80.8 all-gather.4
  92.1 58.7 all-gather.2
  166.2 103.1 reduce-scatter.1
